TPU v7x, 32 devices: a whole 2x2x4 slice. The times are simulated.
32 devices in a mesh: groups: 1, seq: 32 (over z, y, x, core).
Axes of the slice: x: 2, y: 2, z: 4, core: 2. Of those that a mesh axis runs over, the one named last changes fastest.
Arguments:
- tokens: bfloat16 [4096, 1536], P(('groups', 'seq')), may hold values from -6 to 6
- state_rates: float32 [2, 64], replicated, may hold values from -40 to 40, as said below
- coupling: float32 [2, 64], replicated, may hold values from -6 to 6
- in_proj: float32 [2, 64, 1536], replicated, may hold values from -120 to 120
- out_proj: float32 [2, 64, 1536], replicated, may hold values from -0.01171875 to 0.01171875
- skip_gain: float32 [1536], replicated, may hold values from -4 to 4
- mix_weight: bfloat16 [1536, 3072], P('seq'), may hold values from -0.15625 to 0.15625
Outputs:
- glu_output: bfloat16 [4096, 1536], P(('groups', 'seq'))
Inputs may be any that keep to these rules, and one draw needn't show every extreme that they name: state_rates[0] is negative, between -12 and -1 / 4096; state_rates[1] lies within -40 to 40.
All inputs are finite; a program needn't handle non-finite values.
Results may differ from a plain program's by a relative error of at most 0.0051.
Values may be sent and summed in bfloat16 or wider, within the bound.
No kernel may reach another device: no remote copies, remote signals or barrier semaphores. Data moves between devices by JAX's collectives and lax.ppermute only.
A program may use at most 64 MiB of HBM per device.

v0:
```python
import math
import jax
import jax.numpy as jnp
from jax import lax
from jax.sharding import PartitionSpec as P

PRECISE = lax.Precision.HIGHEST


def phase_of(numerator, period):
    wrapped = numerator % period
    wrapped = jnp.where(wrapped > period // 2, wrapped - period, wrapped)
    return wrapped.astype(jnp.float32) * (-2.0 * math.pi / period)


def complex_mul(first, second):
    return (
        first[0] * second[0] - first[1] * second[1],
        first[0] * second[1] + first[1] * second[0],
    )


def complex_div(first, second):
    norm_sq = second[0] * second[0] + second[1] * second[1]
    return (
        (first[0] * second[0] + first[1] * second[1]) / norm_sq,
        (first[1] * second[0] - first[0] * second[1]) / norm_sq,
    )


def real_form(pair_real, pair_imag):
    upper = jnp.concatenate([pair_real, pair_imag], axis=1)
    lower = jnp.concatenate([-pair_imag, pair_real], axis=1)
    return jnp.concatenate([upper, lower], axis=0)


def cauchy_right(coupling, in_proj, out_proj):
    in_pair = (in_proj[0], in_proj[1])
    out_pair = (out_proj[0], out_proj[1])
    low_pair = (coupling[0][:, None], coupling[1][:, None])
    low_conj = (low_pair[0], -low_pair[1])
    pair_cb = complex_mul(out_pair, in_pair)
    pair_cp = complex_mul(out_pair, low_pair)
    pair_pb = complex_mul(low_conj, in_pair)
    pair_pp = low_pair[0] * low_pair[0] + low_pair[1] * low_pair[1]
    return [
        real_form(pair_cb[0], pair_cb[1]),
        real_form(pair_cp[0], pair_cp[1]),
        real_form(pair_pb[0], pair_pb[1]),
        real_form(pair_pp, jnp.zeros_like(pair_pp)),
    ]


def response(frequency, full_len, state_rates, right_list):
    half_turn = 0.5 * phase_of(frequency, full_len)
    cos_half = jnp.cos(half_turn)[:, None]
    sin_half = jnp.sin(half_turn)[:, None]
    decay_rate = -state_rates[0][None, :]
    spin_rate = state_rates[1][None, :]
    real_part = cos_half * decay_rate
    imag_part = -(2.0 * sin_half + cos_half * spin_rate)
    inv_norm = 1.0 / (real_part * real_part + imag_part * imag_part)
    cauchy_left = jnp.concatenate([real_part * inv_norm, -imag_part * inv_norm], axis=1)
    term_list = []
    for matrix in right_list:
        summed = jnp.dot(cauchy_left, matrix, precision=PRECISE)
        half_cols = matrix.shape[1] // 2
        term_list.append((summed[:, :half_cols], summed[:, half_cols:]))
    term_cb, term_cp, term_pb, term_pp = term_list
    numerator = complex_mul(term_cp, term_pb)
    denominator = (1.0 + cos_half * term_pp[0], cos_half * term_pp[1])
    fraction = complex_div(numerator, denominator)
    bracket = (term_cb[0] - cos_half * fraction[0], term_cb[1] - cos_half * fraction[1])
    return complex_mul((cos_half, -sin_half), bracket)


def dft_table_of(length, direction):
    position = jnp.arange(length, dtype=jnp.int32)
    phases = phase_of(direction * position[:, None] * position[None, :], length)
    cos_table = jnp.cos(phases)
    sin_table = jnp.sin(phases)
    return jnp.stack(
        [jnp.stack([cos_table, -sin_table], 1), jnp.stack([sin_table, cos_table], 1)], 0
    )


def transform(signal, length, direction):
    return jnp.einsum("ascb,ckbh->aksh", dft_table_of(length, direction), signal, precision=PRECISE)


def block_tables(seq_count):
    block_index = jnp.arange(seq_count, dtype=jnp.int32)
    pair_index = jnp.arange(2 * seq_count, dtype=jnp.int32)
    forward_phase = phase_of(pair_index[:, None] * block_index[None, :], 2 * seq_count)
    forward_table = jnp.concatenate([jnp.cos(forward_phase), jnp.sin(forward_phase)], 0)
    inverse_phase = phase_of(-(block_index[:, None] * pair_index[None, :]), 2 * seq_count)
    inverse_table = jnp.concatenate([jnp.cos(inverse_phase), -jnp.sin(inverse_phase)], 1)
    return (forward_table, inverse_table)


def twiddled(signal, first_index, second_index, full_len, direction):
    phases = phase_of(direction * first_index[:, None] * second_index[None, :], full_len)[
        :, :, None
    ]
    turned = complex_mul((signal[0], signal[1]), (jnp.cos(phases), jnp.sin(phases)))
    return jnp.stack(turned)


def shards(tokens, state_rates, coupling, in_proj, out_proj, skip_gain, mix_weight):
    seq_count = lax.axis_size("seq")
    seq_place = lax.axis_index("seq")
    tok_rows, channels = tokens.shape
    full_len = 2 * tok_rows * seq_count
    forward_table, inverse_table = block_tables(seq_count)
    pair_index = jnp.arange(2 * seq_count, dtype=jnp.int32)
    all_times = jnp.arange(tok_rows, dtype=jnp.int32)
    per_device = tok_rows // seq_count
    columns = lax.all_to_all(tokens[None], "seq", split_axis=1, concat_axis=0, tiled=True)
    spread = jnp.dot(
        forward_table,
        columns.astype(jnp.float32).reshape(seq_count, per_device * channels),
        precision=PRECISE,
    )
    spread = spread.reshape(2, 2 * seq_count, per_device, channels)
    local_time = seq_place * per_device + jnp.arange(per_device, dtype=jnp.int32)
    spread = twiddled(spread, pair_index, local_time, full_len, 1)
    gathered = lax.all_to_all(spread, "seq", split_axis=1, concat_axis=2, tiled=True)
    spectrum = transform(gathered, tok_rows, 1)
    pair_here = 2 * seq_place + jnp.arange(2, dtype=jnp.int32)
    frequency = (pair_here[:, None] + 2 * seq_count * all_times[None, :]).reshape(-1)
    right_list = cauchy_right(coupling, in_proj, out_proj)
    kernel_real, kernel_imag = response(frequency, full_len, state_rates, right_list)
    kernel_pair = (
        kernel_real.reshape(2, tok_rows, channels),
        kernel_imag.reshape(2, tok_rows, channels),
    )
    product = jnp.stack(complex_mul(kernel_pair, (spectrum[0], spectrum[1])))
    inverse = transform(product, tok_rows, -1)
    inverse = twiddled(inverse, pair_here, all_times, full_len, -1)
    returned = lax.all_to_all(inverse, "seq", split_axis=2, concat_axis=1, tiled=True)
    conv_out = jnp.dot(
        inverse_table, returned.reshape(4 * seq_count, per_device * channels), precision=PRECISE
    )
    conv_out = conv_out.reshape(seq_count, per_device, channels) * (1.0 / full_len)
    pre_act = conv_out + skip_gain * columns.astype(jnp.float32)
    activation = jax.nn.gelu(pre_act, approximate=False).astype(jnp.bfloat16)
    act_rows = lax.all_to_all(activation, "seq", split_axis=0, concat_axis=1, tiled=True)[0]
    projected = jnp.dot(
        act_rows,
        lax.all_gather(mix_weight, "seq", axis=0, tiled=True),
        preferred_element_type=jnp.float32,
    )
    return (projected[:, :channels] * jax.nn.sigmoid(projected[:, channels:])).astype(jnp.bfloat16)


def solution(mesh):
    placed = (P(("groups", "seq"), None), P(), P(), P(), P(), P(), P("seq", None))
    return jax.shard_map(
        shards, mesh=mesh, in_specs=placed, out_specs=P(("groups", "seq"), None), check_vma=False
    )
```

profile of v0, /device:TPU:0, one launch (start us, length us, event | category | flops | bytes accessed | tf_op | source)
XLA Modules:
  0.0 290.9 jit_solution(13883926220681180937)
XLA Ops:
  8.7 3.0 %reduce.4 = bf16[128,1536]{1,0:T(8,128)(2,1)S(1)} reduce(bf16[128,1,1536]{2,1,0:T(2,128)(2,1)S(1)} %bitcast.155, bf16[]{:T(256)} %broadcast.842), dimensions={1}, to_apply=%bitcast.146.reduce_sub_computation | reduce | bytes 786434
  12.7 7.3 %all-to-all-start = ((bf16[32,2,3072]{2,1,0:T(2,128)(2,1)}), bf16[32,2,3072]{2,1,0:T(2,128)(2,1)S(1)}, u32[]{:S(2)}, u32[]{:S(2)}) async-start(bf16[32,2,3072]{2,1,0:T(2,128)(2,1)} %reshape.574), calls=%async_computation | async-start | bytes 786432 | tf_op jit(solution)/shard_map/all_to_all | solution.py:118
  21.2 12.1 %all-to-all-done = bf16[32,2,3072]{2,1,0:T(2,128)(2,1)S(1)} async-done(((bf16[32,2,3072]{2,1,0:T(2,128)(2,1)}), bf16[32,2,3072]{2,1,0:T(2,128)(2,1)S(1)}, u32[]{:S(2)}, u32[]{:S(2)}) %all-to-all-start) | async-done | bytes 393248 | tf_op jit(solution)/shard_map/all_to_all | solution.py:118
  40.1 2.4 squeeze.30
  43.3 2.5 pad_maximum_fusion
  45.8 3.1 %all-to-all-start.1 = ((f32[2,64,4,1536]{3,2,0,1:T(4,128)}), f32[2,64,4,1536]{3,2,0,1:T(4,128)S(1)}, u32[]{:S(2)}, u32[]{:S(2)}) async-start(f32[2,64,4,1536]{3,2,0,1:T(4,128)} %pad_maximum_fusion), calls=%async_computation.1 | async-start | bytes 6291456 | tf_op jit(solution)/shard_map/all_to_all | solution.py:127
  51.1 2.7 fusion.12
  53.8 2.7 fusion.20
  56.5 2.7 fusion.4
  63.5 3.0 %copy.80 = f32[1,2,128,1536]{2,3,0,1:T(8,128)} copy(f32[1,2,128,1536]{3,2,1,0:T(8,128)} %bitcast.152) | data formatting | bytes 3145728 | tf_op jit(solution)/shard_map/reshape | solution.py:135
  66.6 3.0 %copy.79 = f32[1,2,128,1536]{2,3,0,1:T(8,128)} copy(f32[1,2,128,1536]{3,2,1,0:T(8,128)} %bitcast.153) | data formatting | bytes 3145728 | tf_op jit(solution)/shard_map/reshape | solution.py:134
  71.3 86.4 %all-to-all-done.1 = f32[2,64,4,1536]{3,2,0,1:T(4,128)S(1)} async-done(((f32[2,64,4,1536]{3,2,0,1:T(4,128)}), f32[2,64,4,1536]{3,2,0,1:T(4,128)S(1)}, u32[]{:S(2)}, u32[]{:S(2)}) %all-to-all-start.1) | async-done | bytes 3145760 | tf_op jit(solution)/shard_map/all_to_all | solution.py:127
  157.7 2.6 copy.77
  160.4 5.1 %convolution_bitcast_fusion.1 = f32[2,2,128,1536]{2,3,0,1:T(8,128)S(1)} fusion(f32[2,2,128,1536,1]{3,1,2,0,4:T(2,128)S(1)} %bitcast.149, f32[1,128,2,128]{3,1,2,0:T(8,128)S(1)} %get-tuple-element.41, f32[1,128,2,128]{3,1,2,0:T(8,128)S(1)} %get-tuple-element.40), kind=kOutput, calls=%fused_computation.1 | convolution fusion | flops 2415984640 | bytes 6553600 | tf_op jit(solution)/shard_map/ascb,ckbh->aksh/dot_general | solution.py:88
  166.4 2.8 convolution_bitcast_fusion
  169.8 3.6 %copy.83 = f32[2,2,128,1536]{3,0,1,2:T(2,128)} copy(f32[2,2,128,1536]{2,3,0,1:T(8,128)S(1)} %pad_maximum_fusion.1) | data formatting | bytes 6291456 | tf_op jit(solution)/shard_map/stack | solution.py:106
  173.3 3.8 %all-to-all-start.2 = ((f32[2,2,128,1536]{3,0,1,2:T(2,128)}), f32[2,2,128,1536]{3,0,1,2:T(2,128)S(1)}, u32[]{:S(2)}, u32[]{:S(2)}) async-start(f32[2,2,128,1536]{3,0,1,2:T(2,128)} %copy.83), calls=%async_computation.2 | async-start | bytes 6291456 | tf_op jit(solution)/shard_map/all_to_all | solution.py:140
  177.3 4.3 %convert_reduce_fusion = f32[128,1536]{1,0:T(8,128)} fusion(bf16[128,1,1536]{2,1,0:T(2,128)(2,1)} %copy-done), kind=kLoop, calls=%fused_computation.60 | loop fusion | flops 196608 | bytes 1179648 | tf_op jit(solution)/shard_map/convert_element_type | solution.py:121
  181.5 2.3 reshape.564
  183.8 64.7 %all-to-all-done.2 = f32[2,2,128,1536]{3,0,1,2:T(2,128)S(1)} async-done(((f32[2,2,128,1536]{3,0,1,2:T(2,128)}), f32[2,2,128,1536]{3,0,1,2:T(2,128)S(1)}, u32[]{:S(2)}, u32[]{:S(2)}) %all-to-all-start.2) | async-done | bytes 3145760 | tf_op jit(solution)/shard_map/all_to_all | solution.py:140
  250.7 2.4 copy.86
  253.1 6.9 %fusion.32 = bf16[32,4,1536]{2,0,1:T(8,128)(2,1)S(1)} fusion(f32[32,4,1536]{2,1,0:T(4,128)} %reshape.564, f32[4,1536,128]{2,1,0:T(8,128)} %bitcast.154, f32[1536]{0:T(1024)S(1)} %copy-done.6, f32[32,64]{1,0:T(8,128)S(1)} %get-tuple-element.64, f32[32,64]{1,0:T(8,128)S(1)} %get-tuple-element.65), kind=kOutput, calls=%fused_computation.53 | convolution fusion | flops 315363328 | bytes 4347904 | tf_op jit(solution)/shard_map/dot_general | solution.py:141
  260.3 17.1 %all_to_all.51 = bf16[32,4,1536]{2,1,0:T(4,128)(2,1)S(1)} all-to-all(bf16[32,4,1536]{2,1,0:T(4,128)(2,1)S(1)} %copy.88), channel_id=1, replica_groups=mesh['groups'=1,'seq'=32] {'seq'}, dimensions={0} | all-to-all | bytes 786432 | tf_op jit(solution)/shard_map/all_to_all | solution.py:147
  277.5 5.1 %fusion.143 = f32[128,3072]{1,0:T(8,128)S(1)} fusion(bf16[128,1536]{1,0:T(8,128)(2,1)S(1)} %squeeze.31, bf16[1536,3072]{1,0:T(8,128)(2,1)} %all-gather.2.cloned.1.call-done), kind=kOutput, calls=%fused_computation.245 | convolution fusion | flops 1207959552 | bytes 11403264 | tf_op jit(solution)/shard_map/dot_general | solution.py:148
  (63 shorter events, 25.1 us)
Async XLA Ops:
  8.7 12.5 %copy-start.4 = (f32[2,64]{1,0:T(2,128)S(1)}, f32[2,64]{1,0:T(2,128)}, u32[]{:S(2)}) copy-start(f32[2,64]{1,0:T(2,128)} %param.8) | copy-start | bytes 1540
  12.7 20.6 %all-to-all-start = ((bf16[32,2,3072]{2,1,0:T(2,128)(2,1)}), bf16[32,2,3072]{2,1,0:T(2,128)(2,1)S(1)}, u32[]{:S(2)}, u32[]{:S(2)}) async-start(bf16[32,2,3072]{2,1,0:T(2,128)(2,1)} %reshape.574), calls=%async_computation | async-start | bytes 786432 | tf_op jit(solution)/shard_map/all_to_all | solution.py:118
  20.0 257.5 %all-gather.2.cloned.1.call-start = ((), (), s32[]{:S(2)}) async-start(), calls=%async_computation.4 | async-start | bytes 9732096 | tf_op jit(solution)/shard_map/all_gather | solution.py:150
  33.6 4.0 %copy-start = (bf16[128,1,1536]{2,1,0:T(2,128)(2,1)}, bf16[128,1,1536]{2,1,0:T(2,128)(2,1)S(1)}, u32[]{:S(2)}) copy-start(bf16[128,1,1536]{2,1,0:T(2,128)(2,1)S(1)} %reshape.575) | copy-start | bytes 1179652
  45.7 3.1 %copy-start.5 = (f32[2,64]{1,0:T(2,128)S(1)}, f32[2,64]{1,0:T(2,128)}, u32[]{:S(2)}) copy-start(f32[2,64]{1,0:T(2,128)} %param.9) | copy-start | bytes 1540
  45.8 112.0 %all-to-all-start.1 = ((f32[2,64,4,1536]{3,2,0,1:T(4,128)}), f32[2,64,4,1536]{3,2,0,1:T(4,128)S(1)}, u32[]{:S(2)}, u32[]{:S(2)}) async-start(f32[2,64,4,1536]{3,2,0,1:T(4,128)} %pad_maximum_fusion), calls=%async_computation.1 | async-start | bytes 6291456 | tf_op jit(solution)/shard_map/all_to_all | solution.py:127
  160.4 5.1 %copy-start.1 = (f32[1,2,128,1536]{2,3,0,1:T(8,128)S(1)}, f32[1,2,128,1536]{2,3,0,1:T(8,128)}, u32[]{:S(2)}) copy-start(f32[1,2,128,1536]{2,3,0,1:T(8,128)} %copy.80) | copy-start | bytes 4718596
  160.4 5.1 %copy-start.2 = (f32[1,2,128,1536]{2,3,0,1:T(8,128)S(1)}, f32[1,2,128,1536]{2,3,0,1:T(8,128)}, u32[]{:S(2)}) copy-start(f32[1,2,128,1536]{2,3,0,1:T(8,128)} %copy.79) | copy-start | bytes 4718596
  165.5 0.9 copy-start.3
  173.3 75.2 %all-to-all-start.2 = ((f32[2,2,128,1536]{3,0,1,2:T(2,128)}), f32[2,2,128,1536]{3,0,1,2:T(2,128)S(1)}, u32[]{:S(2)}, u32[]{:S(2)}) async-start(f32[2,2,128,1536]{3,0,1,2:T(2,128)} %copy.83), calls=%async_computation.2 | async-start | bytes 6291456 | tf_op jit(solution)/shard_map/all_to_all | solution.py:140
  250.7 2.4 copy-start.6
Sparse Core Ops, SparseCore 0:
  23.7 128.8 all-gather.1
where the time goes:
time: 295 us; the launch traced here: 291 us
  waiting for transfers between devices  163 us (55%)
  local copies, waits for them, and re-layouts  31.1 us (11%)
  matrix products  29.7 us (10%)
  other arithmetic  20.6 us (7%)
  blocking collectives  17.1 us (6%)
  starting transfers between devices  14.7 us (5%)
  between operations  14.2 us (5%)
    all_to_all x1, waiting for transfers between devices, shards(): lax.all_to_all(spread, 'seq', split_axis=1, concat_axis=2, tiled=True)  86.4 us
    all_to_all x1, waiting for transfers between devices, shards(): lax.all_to_all(inverse, 'seq', split_axis=2, concat_axis=1, tiled=True)  64.7 us
    all_to_all x1, blocking collectives, shards(): lax.all_to_all(activation, 'seq', split_axis=0, concat_axis=1, tiled=True)  17.1 us
    all_to_all x1, waiting for transfers between devices, shards(): lax.all_to_all(tokens[None], 'seq', split_axis=1, concat_axis=0, tiled=True)  12.1 us
    dot_general x4, matrix products, response(): summed = jnp.dot(cauchy_left, matrix, precision=PRECISE)  8.33 us
    dot_general x2, matrix products, transform(): jnp.einsum('ascb,ckbh->aksh', dft_table_of(length, direction), signal, pr...  7.88 us
    all_to_all x1, starting transfers between devices, shards(): lax.all_to_all(tokens[None], 'seq', split_axis=1, concat_axis=0, tiled=True)  7.33 us
    dot_general x1, matrix products, shards(): jnp.dot(inverse_table, returned.reshape(4 * seq_count, per_device * chann...  6.92 us
  transfers between devices with their start and end apart: 4, of which 3 were waited for; matrix products, arithmetic and copies ran while one was open for 24% of the time, Pallas kernels for 0%

commit v1 on v0

--- a/solution.py
+++ b/solution.py
@@ -137,7 +137,10 @@
     product = jnp.stack(complex_mul(kernel_pair, (spectrum[0], spectrum[1])))
     inverse = transform(product, tok_rows, -1)
     inverse = twiddled(inverse, pair_here, all_times, full_len, -1)
-    returned = lax.all_to_all(inverse, "seq", split_axis=2, concat_axis=1, tiled=True)
+    returned = jnp.concatenate(
+        lax.all_to_all(jnp.stack(jnp.split(inverse, lax.axis_size("seq"), axis=2)), "seq", 0, 0),
+        axis=1,
+    )
     conv_out = jnp.dot(
         inverse_table, returned.reshape(4 * seq_count, per_device * channels), precision=PRECISE
     )

time: 295 us -> 311 us (1.054)
  other arithmetic: 20.6 us -> 41.5 us
  local copies, waits for them, and re-layouts: 31.1 us -> 26.7 us
    unnamed x1 -> x32, other arithmetic: 3.01 us -> 23.2 us
    another operation x1 -> x0, local copies, waits for them, and re-layouts: 3.57 us -> none  [twiddled(): return jnp.stack(turned)]
  transfers between devices with their start and end apart: 4 -> 4, of which waited for: 3 -> 3; matrix products, arithmetic and copies ran while one was open for 24% -> 28% of each run, Pallas kernels for 0% -> 0%
where the time goes in v1:
time: 311 us; the launch traced here: 307 us
  waiting for transfers between devices  163 us (52%)
  other arithmetic  41.5 us (13%)
  matrix products  29.9 us (10%)
  local copies, waits for them, and re-layouts  26.7 us (9%)
  blocking collectives  17.1 us (5%)
  starting transfers between devices  14.6 us (5%)
  between operations  14.2 us (5%)
    all_to_all x1, waiting for transfers between devices, shards(): lax.all_to_all(spread, 'seq', split_axis=1, concat_axis=2, tiled=True)  86.4 us
    all_to_all x1, waiting for transfers between devices, shards(): lax.all_to_all(jnp.stack(jnp.split(inverse, lax.axis_size('seq'), axis=2)...  64.7 us
    unnamed x32, other arithmetic  23.2 us
    all_to_all x1, blocking collectives, shards(): lax.all_to_all(activation, 'seq', split_axis=0, concat_axis=1, tiled=True)  17.1 us
    all_to_all x1, waiting for transfers between devices, shards(): lax.all_to_all(tokens[None], 'seq', split_axis=1, concat_axis=0, tiled=True)  12.1 us
    dot_general x4, matrix products, response(): summed = jnp.dot(cauchy_left, matrix, precision=PRECISE)  8.32 us
    dot_general x2, matrix products, transform(): jnp.einsum('ascb,ckbh->aksh', dft_table_of(length, direction), signal, pr...  8.05 us
    all_to_all x1, starting transfers between devices, shards(): lax.all_to_all(tokens[None], 'seq', split_axis=1, concat_axis=0, tiled=True)  7.33 us
  transfers between devices with their start and end apart: 4, of which 3 were waited for; matrix products, arithmetic and copies ran while one was open for 28% of the time, Pallas kernels for 0%

profile of v1, /device:TPU:0, one launch (start us, length us, event | category | flops | bytes accessed | tf_op | source)
XLA Modules:
  0.0 307.3 jit_solution(6931523813743567248)
XLA Ops:
  8.7 3.0 reduce.4
  12.7 7.3 %all-to-all-start = ((bf16[32,2,3072]{2,1,0:T(2,128)(2,1)}), bf16[32,2,3072]{2,1,0:T(2,128)(2,1)S(1)}, u32[]{:S(2)}, u32[]{:S(2)}) async-start(bf16[32,2,3072]{2,1,0:T(2,128)(2,1)} %reshape.573), calls=%async_computation | async-start | bytes 786432 | tf_op jit(solution)/shard_map/all_to_all | solution.py:118
  21.2 12.1 %all-to-all-done = bf16[32,2,3072]{2,1,0:T(2,128)(2,1)S(1)} async-done(((bf16[32,2,3072]{2,1,0:T(2,128)(2,1)}), bf16[32,2,3072]{2,1,0:T(2,128)(2,1)S(1)}, u32[]{:S(2)}, u32[]{:S(2)}) %all-to-all-start) | async-done | bytes 393248 | tf_op jit(solution)/shard_map/all_to_all | solution.py:118
  33.6 2.2 bitcast_reduce_fusion
  40.1 2.4 squeeze.30
  43.3 2.5 pad_maximum_fusion
  45.7 3.1 %all-to-all-start.1 = ((f32[2,64,4,1536]{3,2,0,1:T(4,128)}), f32[2,64,4,1536]{3,2,0,1:T(4,128)S(1)}, u32[]{:S(2)}, u32[]{:S(2)}) async-start(f32[2,64,4,1536]{3,2,0,1:T(4,128)} %pad_maximum_fusion), calls=%async_computation.1 | async-start | bytes 6291456 | tf_op jit(solution)/shard_map/all_to_all | solution.py:127
  51.1 2.7 fusion.12
  53.8 2.7 fusion.20
  56.5 2.7 fusion.4
  63.5 3.0 copy.79
  66.5 3.0 copy.78
  71.3 86.4 %all-to-all-done.1 = f32[2,64,4,1536]{3,2,0,1:T(4,128)S(1)} async-done(((f32[2,64,4,1536]{3,2,0,1:T(4,128)}), f32[2,64,4,1536]{3,2,0,1:T(4,128)S(1)}, u32[]{:S(2)}, u32[]{:S(2)}) %all-to-all-start.1) | async-done | bytes 3145760 | tf_op jit(solution)/shard_map/all_to_all | solution.py:127
  157.7 2.6 copy.76
  160.4 5.1 %convolution_bitcast_fusion.1 = f32[2,2,128,1536]{2,3,0,1:T(8,128)S(1)} fusion(f32[2,2,128,1536,1]{3,1,2,0,4:T(2,128)S(1)} %bitcast.213, f32[1,128,2,128]{3,1,2,0:T(8,128)S(1)} %get-tuple-element.41, f32[1,128,2,128]{3,1,2,0:T(8,128)S(1)} %get-tuple-element.40), kind=kOutput, calls=%fused_computation.63 | convolution fusion | flops 2415984640 | bytes 6553600 | tf_op jit(solution)/shard_map/ascb,ckbh->aksh/dot_general | solution.py:88
  166.4 3.0 convolution_bitcast_fusion
  190.8 3.6 %all-to-all-start.2 = ((f32[32,2,2,4,1536]{4,3,1,2,0:T(4,128)}), f32[32,2,2,4,1536]{4,3,1,2,0:T(4,128)S(1)}, u32[]{:S(2)}, u32[]{:S(2)}) async-start(f32[32,2,2,4,1536]{4,3,1,2,0:T(4,128)} %fusion.87), calls=%async_computation.2 | async-start | bytes 6291456 | tf_op jit(solution)/shard_map/all_to_all | solution.py:141
  194.4 4.3 %convert_reduce_fusion = f32[128,1536]{1,0:T(8,128)} fusion(bf16[128,1,1536]{2,1,0:T(2,128)(2,1)} %copy-done), kind=kLoop, calls=%fused_computation.121 | loop fusion | flops 196608 | bytes 1179648 | tf_op jit(solution)/shard_map/convert_element_type | solution.py:121
  198.7 2.3 reshape.563
  201.0 64.7 %all-to-all-done.2 = f32[32,2,2,4,1536]{4,3,1,2,0:T(4,128)S(1)} async-done(((f32[32,2,2,4,1536]{4,3,1,2,0:T(4,128)}), f32[32,2,2,4,1536]{4,3,1,2,0:T(4,128)S(1)}, u32[]{:S(2)}, u32[]{:S(2)}) %all-to-all-start.2) | async-done | bytes 3145760 | tf_op jit(solution)/shard_map/all_to_all | solution.py:141
  267.2 2.4 copy.84
  269.5 6.9 %fusion.32 = bf16[32,4,1536]{2,0,1:T(8,128)(2,1)S(1)} fusion(f32[32,4,1536]{2,1,0:T(4,128)} %reshape.563, f32[4,1536,128]{2,1,0:T(8,128)} %bitcast.218, f32[1536]{0:T(1024)S(1)} %copy-done.6, f32[32,64]{1,0:T(8,128)S(1)} %get-tuple-element.64, f32[32,64]{1,0:T(8,128)S(1)} %get-tuple-element.65), kind=kOutput, calls=%fused_computation.114 | convolution fusion | flops 315363328 | bytes 4347904 | tf_op jit(solution)/shard_map/dot_general | solution.py:144
  276.8 17.1 %all_to_all.41 = bf16[32,4,1536]{2,1,0:T(4,128)(2,1)S(1)} all-to-all(bf16[32,4,1536]{2,1,0:T(4,128)(2,1)S(1)} %copy.86), channel_id=1, replica_groups=mesh['groups'=1,'seq'=32] {'seq'}, dimensions={0} | all-to-all | bytes 786432 | tf_op jit(solution)/shard_map/all_to_all | solution.py:150
  294.0 5.1 %fusion.176 = f32[128,3072]{1,0:T(8,128)S(1)} fusion(bf16[128,1536]{1,0:T(8,128)(2,1)S(1)} %squeeze.31, bf16[1536,3072]{1,0:T(8,128)(2,1)} %all-gather.2.cloned.1.call-done), kind=kOutput, calls=%fused_computation.371 | convolution fusion | flops 1207959552 | bytes 11403264 | tf_op jit(solution)/shard_map/dot_general | solution.py:151
  (93 shorter events, 43.0 us)
Async XLA Ops:
  6.5 14.6 %copy-start.4 = (f32[2,64]{1,0:T(2,128)S(1)}, f32[2,64]{1,0:T(2,128)}, u32[]{:S(2)}) copy-start(f32[2,64]{1,0:T(2,128)} %param.8) | copy-start | bytes 1540
  12.7 20.6 %all-to-all-start = ((bf16[32,2,3072]{2,1,0:T(2,128)(2,1)}), bf16[32,2,3072]{2,1,0:T(2,128)(2,1)S(1)}, u32[]{:S(2)}, u32[]{:S(2)}) async-start(bf16[32,2,3072]{2,1,0:T(2,128)(2,1)} %reshape.573), calls=%async_computation | async-start | bytes 786432 | tf_op jit(solution)/shard_map/all_to_all | solution.py:118
  20.0 274.0 %all-gather.2.cloned.1.call-start = ((), (), s32[]{:S(2)}) async-start(), calls=%async_computation.4 | async-start | bytes 9732096 | tf_op jit(solution)/shard_map/all_gather | solution.py:153
  33.6 5.4 %copy-start = (bf16[128,1,1536]{2,1,0:T(2,128)(2,1)}, bf16[128,1,1536]{2,1,0:T(2,128)(2,1)S(1)}, u32[]{:S(2)}) copy-start(bf16[128,1,1536]{2,1,0:T(2,128)(2,1)S(1)} %reshape.574) | copy-start | bytes 1179652
  45.7 3.1 %copy-start.5 = (f32[2,64]{1,0:T(2,128)S(1)}, f32[2,64]{1,0:T(2,128)}, u32[]{:S(2)}) copy-start(f32[2,64]{1,0:T(2,128)} %param.9) | copy-start | bytes 1540
  45.7 112.0 %all-to-all-start.1 = ((f32[2,64,4,1536]{3,2,0,1:T(4,128)}), f32[2,64,4,1536]{3,2,0,1:T(4,128)S(1)}, u32[]{:S(2)}, u32[]{:S(2)}) async-start(f32[2,64,4,1536]{3,2,0,1:T(4,128)} %pad_maximum_fusion), calls=%async_computation.1 | async-start | bytes 6291456 | tf_op jit(solution)/shard_map/all_to_all | solution.py:127
  160.4 5.1 %copy-start.1 = (f32[1,2,128,1536]{2,3,0,1:T(8,128)S(1)}, f32[1,2,128,1536]{2,3,0,1:T(8,128)}, u32[]{:S(2)}) copy-start(f32[1,2,128,1536]{2,3,0,1:T(8,128)} %copy.79) | copy-start | bytes 4718596
  160.4 5.1 %copy-start.2 = (f32[1,2,128,1536]{2,3,0,1:T(8,128)S(1)}, f32[1,2,128,1536]{2,3,0,1:T(8,128)}, u32[]{:S(2)}) copy-start(f32[1,2,128,1536]{2,3,0,1:T(8,128)} %copy.78) | copy-start | bytes 4718596
  165.5 0.9 copy-start.3
  190.8 74.9 %all-to-all-start.2 = ((f32[32,2,2,4,1536]{4,3,1,2,0:T(4,128)}), f32[32,2,2,4,1536]{4,3,1,2,0:T(4,128)S(1)}, u32[]{:S(2)}, u32[]{:S(2)}) async-start(f32[32,2,2,4,1536]{4,3,1,2,0:T(4,128)} %fusion.87), calls=%async_computation.2 | async-start | bytes 6291456 | tf_op jit(solution)/shard_map/all_to_all | solution.py:141
  267.2 2.4 copy-start.6
Sparse Core Ops, SparseCore 0:
  23.7 128.8 all-gather.1
